TPU v7x, 32 devices: a whole 2x2x4 slice. The times are simulated.
32 devices in a mesh: section: 4 (over y, core), dp: 8 (over z, x).
Axes of the slice: x: 2, y: 2, z: 4, core: 2. Of those that a mesh axis runs over, the one named last changes fastest.
Arguments:
- patches: bfloat16 [16, 197, 768], P('dp'), may hold values from -6 to 6
- page_mask: int32 [16, 197], P('dp'), may hold values from 0 to 1, as said below
- mask_token: bfloat16 [768], replicated, may hold values from -6 to 6
- buckets: int32 [197, 197], replicated, may hold values from 0 to 731
- ln_gain: bfloat16 [4, 768], P('section'), may hold values from 0.25 to 1.75
- ln_shift: bfloat16 [4, 768], P('section'), may hold values from -4 to 4
- layer_scale: bfloat16 [4, 768], P('section'), may hold values from 0.25 to 1.75
- branch_bias: bfloat16 [4, 768], P('section'), may hold values from -4 to 4
- qkv_weight: bfloat16 [2, 768, 2304], P(None, 'dp'), may hold values from -0.21875 to 0.21875
- qv_bias: bfloat16 [2, 1536], replicated, may hold values from -4 to 4
- out_weight: bfloat16 [2, 768, 768], P(None, 'dp'), may hold values from -1.25 to 1.25
- rel_table: bfloat16 [2, 12, 732], replicated, may hold values from -6 to 6
- up_weight: bfloat16 [2, 768, 3072], P(None, 'dp'), may hold values from -0.21875 to 0.21875
- up_bias: bfloat16 [2, 3072], replicated, may hold values from -4 to 4
- down_weight: bfloat16 [2, 3072, 768], P(None, 'dp'), may hold values from -0.109375 to 0.109375
- cotangent: bfloat16 [16, 197, 768], P('dp'), may hold values from -6 to 6
Outputs:
- block_out: bfloat16 [16, 197, 768], P('dp', None, 'section')
- input_grad: float32 [16, 197, 768], P('dp', None, 'section')
- qkv_grad: float32 [2, 768, 2304], P(None, 'dp', 'section')
- out_grad: float32 [2, 768, 768], P(None, 'dp', 'section')
- up_grad: float32 [2, 768, 3072], P(None, 'dp', 'section')
- down_grad: float32 [2, 3072, 768], P(None, 'dp', 'section')
- qv_bias_grad: float32 [2, 1536], replicated
- up_bias_grad: float32 [2, 3072], replicated
- table_grad: float32 [2, 12, 732], replicated
- gain_grad: float32 [4, 768], P('section')
- shift_grad: float32 [4, 768], P('section')
- scale_grad: float32 [4, 768], P('section')
- bias_grad: float32 [4, 768], P('section')
- mask_token_grad: float32 [768], replicated
Inputs may be any that keep to these rules, and one draw needn't show every extreme that they name: `page_mask`: each page masks its patches independently, with a probability of its own drawn per page between 20 and 60 percent.
All inputs are finite; a program needn't handle non-finite values.
Results may differ from a plain program's by a relative error of at most 0.018.
Values may be sent and summed in bfloat16 or wider, within the bound.
A program may use at most 256 MiB of HBM per device.

v0:
```python
import functools
import types

import jax
import jax.numpy as jnp
from jax import lax
from jax.experimental import pallas as pl
from jax.experimental.pallas import tpu as pltpu
from jax.sharding import PartitionSpec as P

EPS = 1e-06
MESH = pl.DeviceIdType.MESH
NEG = -1e30
LANES = 128
BF = jnp.bfloat16
F32 = jnp.float32


def pad_up(x, m):
    return (x + m - 1) // m * m


def nn(a, b):
    return jnp.dot(a, b, preferred_element_type=F32)


def nt(a, b):
    return lax.dot_general(a, b, (((1,), (1,)), ((), ())), preferred_element_type=F32)


def tn(a, b):
    return lax.dot_general(a, b, (((0,), (0,)), ((), ())), preferred_element_type=F32)


class Layout:
    def __init__(self, layers, heads, head, rows, prow, pcol, width, hidden, shard, highs, fused):
        self.layers, self.heads, self.head = layers, heads, head
        self.rows, self.prow, self.pcol, self.width, self.hidden = rows, prow, pcol, width, hidden
        self.shard, self.highs, self.fused = shard, highs, fused
        self.own = heads * head
        self.halves = 2 * layers
        self.scale_at, self.bias_at, self.gain_at, self.shift_at, self.token_at = range(5)
        self.qv_at, self.up_at, self.table_at = 0, layers, 2 * layers
        self.sec_rows = pad_up(2 * layers + layers * heads, 8)


def norm_stats(x):
    mean = jnp.mean(x, -1, keepdims=True)
    centered = x - mean
    r = lax.rsqrt(jnp.mean(centered * centered, -1, keepdims=True) + EPS)
    return centered * r, r


ITEMS = ("qkv", "out", "up", "dn")
QKV, OUT, UP, DN = range(4)


def blocks_kernel(lay, names, *refs):
    r = types.SimpleNamespace(**dict(zip(names, refs)))
    fused = lay.fused
    section = lax.axis_index("section")
    core = lax.rem(section, 2)
    mate_at = section + 1 - 2 * core
    mate = {"section": mate_at}
    far = {"section": lax.rem(section + 2, 4)}
    layers, halves, prow, width = lay.layers, lay.halves, lay.prow, lay.width
    rows, pcol = lay.rows, lay.pcol
    own, hid, hd, heads, shard = lay.own, lay.hidden, lay.head, lay.heads, lay.shard
    v_buf, normed, branch, qkv, probs = r.v_buf, r.normed, r.branch, r.qkv, r.probs
    ctx, act, gate, bgrad, dqkv = r.ctx, r.act, r.gate, r.bgrad, r.dqkv
    acc, g_buf, g4_buf, ds_ref, bias_ref = r.acc, r.g_buf, r.g4_buf, r.ds, r.bias
    tiles, sec, vec_all = r.tiles, r.sec, r.vec_all
    core_out, core_in, far_out, far_in = r.core_out, r.core_in, r.far_out, r.far_in

    def remote(src, dst, send, recv, device):
        return pltpu.make_async_remote_copy(
            src_ref=src, dst_ref=dst, send_sem=send, recv_sem=recv, device_id=device, device_id_type=MESH
        )

    loads = {}

    def load(name, src, dst):
        loads[name] = pltpu.make_async_copy(src, dst, r.load_s.at[len(loads)])
        loads[name].start()

    def loaded(*wanted):
        for name in wanted:
            loads[name].wait()

    if fused:
        load("qkv", r.qkv_weight, r.raw_qkv)
        for n, name in enumerate(("ln_gain", "ln_shift", "layer_scale", "branch_bias")):
            load(name, getattr(r, name), r.raw_vec.at[n])
        load("up", r.up_weight, r.raw_up)
        load("qv_bias", r.qv_bias, r.raw_qvb)
        load("up_bias", r.up_bias, r.raw_upb)
    load("patches", r.patches, r.raw_x)
    load("mask", r.page_mask, r.raw_mask)
    load("token", r.mask_token, r.raw_token)
    load("buckets", r.buckets, r.raw_ids)
    load("table", r.rel_table, r.raw_table)
    load("cotangent", r.cotangent, r.raw_g)

    partners = [mate, far]
    if fused:
        dp = lax.axis_index("dp")
        zi, xi = dp // 2, lax.rem(dp, 2)
        xmate = {"dp": zi * 2 + 1 - xi}
        hi, par = zi // 2, lax.rem(zi, 2)
        znear = {"dp": (zi + 1 - 2 * par) * 2 + xi}
        zfar = {"dp": lax.rem(zi + 2, 4) * 2 + xi}
        snext = [lax.rem(section + o, 4) for o in (1, 2, 3)]
        sprev = [lax.rem(section + 4 - o, 4) for o in (1, 2, 3)]
        sdev = [{"section": t} for t in snext]
        partners = [xmate, znear, zfar] + sdev

    barrier = pltpu.get_barrier_semaphore()
    for other in partners:
        pl.semaphore_signal(barrier, inc=1, device_id=other, device_id_type=MESH)

    sends = []

    def sent(copy, when=None):
        sends.append((copy, when))

    def each_section(body):
        for t in range(4):
            pl.when(section == t)(functools.partial(body, t))

    if fused:
        zfs, zfr, zns, znr = r.ag_zfs, r.ag_zfr, r.ag_zns, r.ag_znr
        xs, xr, ls = r.ag_xs, r.ag_xr, r.ag_ls
        my_out = zi == section
        out_far = lax.rem(section + 2, 4) == zi
        out_even = lax.rem(section + zi, 2) == 0
        out_odd = jnp.logical_not(out_even)

        def item(n):
            l, kind = n // 4, ITEMS[n % 4]
            if kind == "out":
                src = r.out_weight.at[l]
            elif kind == "dn":
                src = r.down_weight.at[l, pl.ds(pl.multiple_of(section * shard, shard), shard)]
            else:
                src = getattr(r, "a_" + kind).at[l]
            return l, kind, src, getattr(r, "w_" + kind)

        def own_copy(n):
            l, kind, src, dst = item(n)
            place = dst.at[l, xi] if kind == "out" else dst.at[l, hi, par, xi]
            return pltpu.make_async_copy(src, place, ls.at[n])

        def far_copy(n):
            l, kind, src, dst = item(n)
            place = dst.at[l, xi] if kind == "out" else dst.at[l, hi, par, xi]
            return remote(src, place, zfs.at[n], zfr.at[n], zfar)

        def near_copy(n):
            l, kind, src, dst = item(n)
            place = dst.at[l, xi] if kind == "out" else dst.at[l, :, par, xi]
            return remote(place, place, zns.at[n], znr.at[n], znear)

        def across(n, stage):
            l, kind, src, dst = item(n)
            if kind == "out":
                place = dst.at[l, xi]
                return remote(src if stage == 0 else place, place, xs.at[n, 0], xr.at[n, 0], xmate)
            place = dst.at[l, :, 1 - par, xi] if stage == 2 else dst.at[l, hi if stage == 0 else 1 - hi, par, xi]
            return remote(src if stage == 0 else place, place, xs.at[n, stage], xr.at[n, stage], xmate)

        def begin(copy, when=None):
            if when is None:
                copy.start()
            else:
                pl.when(when)(copy.start)

        def both_ends(copy, when=None):
            begin(copy, when)
            sent(copy, when)

        def gather_start(n):
            if n >= 4 * layers:
                return
            when = my_out if n % 4 == OUT else None
            both_ends(far_copy(n), when)
            begin(own_copy(n), when)

        def gather_across(n):
            if n >= 4 * layers:
                return
            if n % 4 == OUT:
                begin(across(n, 0), my_out)
                sent(across(n, 0))
            else:
                both_ends(across(n, 0))

        def pump_far(n):
            if n % 4 == OUT:

                @pl.when(out_far)
                def _():
                    far_copy(n).wait_recv()
                    across(n, 1).start()

                pl.when(my_out)(own_copy(n).wait)
                both_ends(near_copy(n), out_even)
                return
            own_copy(n).wait()
            far_copy(n).wait_recv()
            both_ends(near_copy(n))
            both_ends(across(n, 1))

        def pump_near(n):
            if n % 4 == OUT:

                @pl.when(out_odd)
                def _():
                    near_copy(n).wait_recv()
                    across(n, 2).start()

                return
            near_copy(n).wait_recv()
            both_ends(across(n, 2))

        def need(n):
            for stage in range(1 if n % 4 == OUT else 3):
                across(n, stage).wait_recv()

        loaded("qkv")

        def slice_qkv(t):
            for l in range(layers):
                parts = [r.raw_qkv[l, :, m * width + t * own : m * width + (t + 1) * own] for m in range(3)]
                r.a_qkv[l] = jnp.concatenate(parts, 1)

        each_section(slice_qkv)
        loaded("ln_gain", "ln_shift", "layer_scale", "branch_bias")
        vec_own = r.vec_own
        vec_own[...] = jnp.zeros_like(vec_own)
        for n in range(4):
            vec_own[n : n + 1, :] = r.raw_vec[n].astype(F32)
        vec_all[section] = vec_own[...]

        pl.semaphore_wait(barrier, len(partners))

        gather_start(QKV)
        gather_across(QKV)
        for o in range(3):
            copy = remote(vec_own, vec_all.at[section], r.vec_s.at[o], r.vec_r.at[o], sdev[o])
            copy.start()
            sent(copy)
        gather_start(OUT)
        gather_across(OUT)
        loaded("up", "up_bias", "qv_bias")
        unit = own // 2

        def slice_up(t):
            for l in range(layers):
                at = [d * 4 * unit + t * unit for d in range(hid // unit)]
                r.a_up[l] = jnp.concatenate([r.raw_up[l, :, a : a + unit] for a in at], 1)
            r.upb[...] = jnp.concatenate([r.raw_upb[:, a : a + unit].astype(F32) for a in at], 1)
            q = r.raw_qvb[:, t * own : (t + 1) * own].astype(F32)
            v = r.raw_qvb[:, width + t * own : width + (t + 1) * own].astype(F32)
            r.qvb[...] = jnp.concatenate([q, jnp.zeros_like(q), v], 1)

        each_section(slice_up)
        gather_start(UP)
        gather_across(UP)
        gather_across(DN)
    else:
        need = pump_far = pump_near = gather_start = gather_across = lambda n: None
        pl.semaphore_wait(barrier, len(partners))

    def weight(kind, l):
        w = getattr(r, "w_" + kind)[l]
        return w.reshape(-1, w.shape[-1])

    tiles[...] = jnp.zeros_like(tiles)
    sec[...] = jnp.zeros_like(sec)
    loaded("patches", "mask", "token")
    mask_row = (r.raw_mask[0:1, :] * (1 - core) + r.raw_mask[1:2, :] * core).astype(F32)
    at_row = lax.broadcasted_iota(jnp.int32, (prow, rows), 0)
    at_column = lax.broadcasted_iota(jnp.int32, (prow, rows), 1)
    mask = jnp.sum(jnp.where(at_row == at_column, mask_row, 0.0), 1, keepdims=True)
    masked = mask > 0.5
    v_buf[0, prow - 16 :, :] = jnp.zeros((16, width), BF)
    token = r.raw_token[...].reshape(1, width).astype(F32)

    def own_page(ref):
        return jnp.where(core == 0, ref[:, 0, :].astype(F32), ref[:, 1, :].astype(F32))

    v_buf[0, :rows, :] = jnp.where(masked[:rows], token, own_page(r.raw_x)).astype(BF)

    def column_sum(x):
        return jnp.sum(x, 0, keepdims=True)

    def vec(kind, k):
        return vec_all[k, kind : kind + 1, :]

    def share_rows(ref, step):
        return remote(ref.at[0], ref.at[1], r.row_s.at[step], r.row_r.at[step], mate)

    def to_mate(step):
        slot = step % 3
        return remote(core_out.at[slot], core_in.at[slot], r.core_s.at[step], r.core_r.at[step], mate)

    def to_far(step):
        slot = step % 3
        return remote(far_out.at[slot], far_in.at[slot], r.far_s.at[step], r.far_r.at[step], far)

    def sum_up_start(step, part):
        core_out[step % 3] = part(1).astype(BF)
        to_mate(step).start()
        acc[...] = part(0)
        to_mate(step).wait_recv()
        far_out[step % 3] = (acc[...] + core_in[step % 3].astype(F32)).astype(BF)
        to_far(step).start()

    def sum_up_end(step):
        to_far(step).wait_recv()
        total = far_out[step % 3].astype(F32) + far_in[step % 3].astype(F32)
        to_mate(step).wait_send()
        to_far(step).wait_send()
        return total

    def norm_row(k):
        xhat, _ = norm_stats(v_buf[k].astype(F32))
        normed[k, 0] = (xhat * vec(0, k) + vec(1, k)).astype(BF)
        share_rows(normed.at[k], k).start()

    def rows_here(ref, step):
        share_rows(ref, step).wait_recv()

    scale = hd ** -0.5

    def attention_page(l, k, slot):
        fresh = nn(normed[k, slot], weight("qkv", l)) + r.qvb[l : l + 1, :]
        qkv[l, slot] = fresh.astype(BF)
        for h in range(heads):
            q = qkv[l, slot, :, h * hd : (h + 1) * hd]
            kk = qkv[l, slot, :, own + h * hd : own + (h + 1) * hd]
            vv = qkv[l, slot, :, 2 * own + h * hd : 2 * own + (h + 1) * hd]
            s = nt(q, kk) * scale + bias_ref[l * heads + h, :, :prow].astype(F32)
            e = jnp.exp(s - jnp.max(s, -1, keepdims=True))
            p = (e / jnp.sum(e, -1, keepdims=True)).astype(BF)
            probs[l, slot, h] = p
            ctx[l, slot, :, h * hd : (h + 1) * hd] = nn(p, vv).astype(BF)

    def mlp_page(l, k, slot):
        pre = nn(normed[k, slot], weight("up", l)) + r.upb[l : l + 1, :]
        c0, c1 = 0.7978845608028654, 0.044715
        square = pre * pre
        t = jnp.tanh(c0 * (pre + c1 * pre * square))
        act[l, slot] = (0.5 * pre * (1.0 + t)).astype(BF)
        slope = 0.5 * (1.0 + t) + 0.5 * pre * (1.0 - t * t) * (c0 * (1.0 + 3.0 * c1 * square))
        gate[l, slot] = slope.astype(BF)

    def end_forward(k, step):
        b = sum_up_end(step) + vec(3, k)
        branch[k] = b
        return (v_buf[k].astype(F32) + vec(2, k) * b).astype(BF)

    def context_part(l):
        return lambda slot: nn(ctx[l, slot], weight("out", l))

    def hidden_part(l):
        return lambda slot: nn(act[l, slot], weight("dn", l))

    cols = own
    if fused:
        def z_first(n):
            return n in (OUT, 4 + DN)

        def first_copy(n):
            l, kind = n // 4, ITEMS[n % 4]
            part, place = getattr(r, "g_" + kind), getattr(r, "x_" + kind)
            if kind == "out":
                src, dst = (part.at[l], place.at[l]) if z_first(n) else (part.at[l, 1 - xi], place.at[l, 0])
            else:
                src, dst = part.at[l, :, 1 - par] if z_first(n) else part.at[l, :, :, 1 - xi], place.at[l]
            return remote(src, dst, r.rs_xs.at[n], r.rs_xr.at[n], znear if z_first(n) else xmate)

        def second_copy(n):
            l, kind = n // 4, ITEMS[n % 4]
            pair, place = getattr(r, "x_" + kind), getattr(r, "n_" + kind)
            if kind == "out":
                src = pair.at[l, 1 - xi] if z_first(n) else pair.at[l, 0]
            else:
                src = pair.at[l, :, 1 - xi] if z_first(n) else pair.at[l, :, 1 - par]
            return remote(src, place.at[l], r.rs_ns.at[n], r.rs_nr.at[n], xmate if z_first(n) else znear)

        def far_sum_copy(n):
            l, kind = n // 4, ITEMS[n % 4]
            four = getattr(r, "n_" + kind)
            src = four.at[l] if kind == "out" else four.at[l, 1 - hi]
            return remote(src, getattr(r, "f_" + kind).at[l], r.rs_fs.at[n], r.rs_fr.at[n], zfar)

        def added(a, b):
            return (a.astype(F32) + b.astype(F32)).astype(BF)

        def sum_start(n):
            both_ends(first_copy(n), out_odd if n % 4 == OUT and z_first(n) else None)

        def sum_first(n):
            l, kind = n // 4, ITEMS[n % 4]
            pair, part = getattr(r, "x_" + kind), getattr(r, "g_" + kind)
            if kind != "out":
                first_copy(n).wait_recv()
                mine = part[l, :, par] if z_first(n) else part[l, :, :, xi]
                pair[l] = added(mine, pair[l])
                both_ends(second_copy(n))
            elif z_first(n):

                @pl.when(out_even)
                def _():
                    first_copy(n).wait_recv()
                    pair[l] = added(part[l], pair[l])

                both_ends(second_copy(n), out_even)
            else:
                first_copy(n).wait_recv()
                pair[l, 0] = added(part[l, xi], pair[l, 0])
                both_ends(second_copy(n), out_odd)

        def sum_second(n):
            l, kind = n // 4, ITEMS[n % 4]
            four, pair = getattr(r, "n_" + kind), getattr(r, "x_" + kind)
            if kind == "out":

                @pl.when(out_even)
                def _():
                    second_copy(n).wait_recv()
                    four[l] = added(pair[l, xi if z_first(n) else 0], four[l])

                both_ends(far_sum_copy(n), out_far)
                return
            second_copy(n).wait_recv()
            four[l] = added(pair[l, :, xi] if z_first(n) else pair[l, :, par], four[l])
            both_ends(far_sum_copy(n))

        def to_section(n, o, src, dst, device):
            return remote(src, dst, r.rs_ss.at[n, o], r.rs_sr.at[n, o], device)

        def finish_item(n):
            l, kind = n // 4, ITEMS[n % 4]
            blocks, got = getattr(r, "s_" + kind), getattr(r, "t_" + kind)
            if kind == "out":

                @pl.when(my_out)
                def _():
                    far_sum_copy(n).wait_recv()
                    total = r.n_out[l].astype(F32) + r.f_out[l].astype(F32)
                    for t in range(4):
                        blocks[l, t] = total[:, t * cols : (t + 1) * cols].astype(BF)
                    for o in range(3):
                        to_section(n, o, blocks.at[l, snext[o]], got.at[l], sdev[o]).start()
                    got[l] = blocks[l, section]

                for o in range(3):
                    sent(to_section(n, o, blocks.at[l, snext[o]], got.at[l], sdev[o]), my_out)
                return
            far_sum_copy(n).wait_recv()
            total = getattr(r, "n_" + kind)[l, hi].astype(F32) + getattr(r, "f_" + kind)[l].astype(F32)
            for t in range(3 if kind == "qkv" else 4):
                blocks[l, t] = total[:, t * cols : (t + 1) * cols].astype(BF)
            if kind == "qkv":
                for m in range(3):
                    at = 4 * m + section
                    dest, place = at // 3, lax.rem(at, 3)
                    away = dest != section
                    copy = remote(
                        blocks.at[l, m], got.at[l, place], r.rs_ss.at[n, m], r.rs_sr.at[n, place], {"section": dest}
                    )
                    pl.when(away)(copy.start)
                    sent(copy, away)

                    @pl.when(jnp.logical_not(away))
                    def _():
                        got[l, place] = blocks[l, m]

                return
            for o in range(3):
                copy = to_section(n, o, blocks.at[l, snext[o]], got.at[l, section], sdev[o])
                copy.start()
                sent(copy)
            got[l, section] = blocks[l, section]

        def item_here(n):
            l, kind = n // 4, ITEMS[n % 4]
            blocks, got = getattr(r, "s_" + kind), getattr(r, "t_" + kind)
            if kind == "out":
                for o in range(3):
                    copy = to_section(n, o, blocks.at[l, 0], got.at[l], sdev[o])
                    pl.when(sprev[o] == zi)(copy.wait_recv)
            elif kind == "qkv":
                for place in range(3):
                    source = lax.rem(3 * section + place, 4)
                    copy = to_section(n, place, blocks.at[l, 0], got.at[l, place], mate)
                    pl.when(source != section)(copy.wait_recv)
            else:
                for o in range(3):
                    to_section(n, o, blocks.at[l, 0], got.at[l, sprev[o]], sdev[o]).wait_recv()

        def share_page(value, name):
            out, place = getattr(r, name), getattr(r, name + "_s")
            for t in range(4):
                place[t] = value[:, t * cols : (t + 1) * cols]
            out[core] = place[section]
            at = int(name == "o_input")
            copy = remote(place.at[mate_at], out.at[core], r.page_s.at[at], r.page_r.at[at], mate)
            copy.start()
            sent(copy)

        def page_here(name):
            at = int(name == "o_input")
            remote(getattr(r, name + "_s").at[0], getattr(r, name).at[1 - core], r.page_s.at[at], r.page_r.at[at], mate).wait_recv()
    else:
        sum_start = sum_first = sum_second = finish_item = lambda n: None

    def keep_grad(n, value):
        ref = getattr(r, "g_" + ITEMS[n % 4])
        ref[n // 4] = value.astype(BF).reshape(ref.shape[1:])

    def table_sums(l, part, parts):
        groups = 2 * heads
        hist = r.hist
        if part == 0:
            hist[...] = jnp.zeros_like(hist)
        step = 8

        def body(block, carry):
            at = pl.multiple_of(block * step, step)
            ids_all = r.ids[pl.ds(at, step), :]
            grads_all = ds_ref[l * groups : (l + 1) * groups, pl.ds(at, step), :]
            total = None
            for row in range(step):
                ids = ids_all[row : row + 1, :]
                low = ids & (LANES - 1)
                high = lax.shift_right_logical(ids, 7)
                spots = lax.broadcasted_iota(jnp.int32, (LANES, pcol), 0)
                hot = jnp.where(spots == low, 1.0, 0.0).astype(BF)
                grads = grads_all[:, row, :]
                parts = [jnp.where(high == number, grads, 0.0) for number in range(lay.highs)]
                got = nt(jnp.concatenate(parts, 0).astype(BF), hot)
                total = got if total is None else total + got
            hist[...] += total
            return carry

        count = pad_up(rows, step) // step
        lax.fori_loop(count * part // parts, count * (part + 1) // parts, body, 0)
        if part + 1 < parts:
            return
        for h in range(heads):
            at = lay.table_at + l * heads + h
            for number in range(lay.highs):
                first = number * groups + 2 * h
                row = hist[first : first + 1, :] + hist[first + 1 : first + 2, :]
                sec[at : at + 1, number * LANES : (number + 1) * LANES] = row

    def make_bias():
        table = r.table
        table[...] = jnp.zeros_like(table)
        count = r.raw_table.shape[2]

        def own_tables(t):
            for l in range(layers):
                for h in range(heads):
                    at = l * heads + h
                    row = r.raw_table[t * heads + h, l : l + 1, :]
                    table[at : at + 1, :count] = row.astype(F32)

        each_section(own_tables)
        ids_ref = r.ids
        ids_ref[...] = jnp.zeros_like(ids_ref)
        ids_ref[:rows, :rows] = r.raw_ids[...]
        step = 16

        def body(block, carry):
            at = pl.multiple_of(block * step, step)
            for half in range(pcol // LANES):
                lanes = slice(half * LANES, (half + 1) * LANES)
                ids = ids_ref[pl.ds(at, step), lanes]
                low = ids & (LANES - 1)
                high = lax.shift_right_logical(ids, 7)
                column = lax.broadcasted_iota(jnp.int32, (step, LANES), 1) + half * LANES
                inside = column < rows
                picks = [high == number for number in range(lay.highs)]
                for t in range(layers * heads):
                    value = jnp.full((step, LANES), NEG, F32)
                    for number in range(lay.highs):
                        row = table[t : t + 1, number * LANES : (number + 1) * LANES]
                        got = jnp.take_along_axis(jnp.broadcast_to(row, (step, LANES)), low, axis=1)
                        value = jnp.where(picks[number], got, value)
                    value = jnp.where(inside, value, NEG)
                    bias_ref[t, pl.ds(at, step), lanes] = value.astype(BF)
            return carry

        lax.fori_loop(0, prow // step, body, 0)

    loaded("buckets", "table", "cotangent")
    make_bias()
    if fused:
        for o in range(3):
            remote(r.vec_own, vec_all.at[sprev[o]], r.vec_s.at[o], r.vec_r.at[o], sdev[o]).wait_recv()

    last = halves - 1

    def branch_grad(k, g):
        step = halves + k
        low = (g * vec(2, k)).astype(BF)
        bgrad[k, 0] = low
        share_rows(bgrad.at[k], step).start()
        tiles[k, lay.bias_at : lay.bias_at + 1, :] = column_sum(low.astype(F32))

    norm_row(0)
    g4_buf[prow - 16 :, :] = jnp.zeros((16, width), F32)
    g4_buf[:rows, :] = own_page(r.raw_g)
    branch_grad(last, g4_buf[...])
    ds_ref[...] = jnp.zeros_like(ds_ref)

    pump_far(QKV)
    gather_across(4 + QKV)
    pump_far(OUT)
    pump_near(QKV)
    gather_across(4 + UP)
    gather_start(DN)
    pump_near(OUT)
    gather_across(4 + OUT)
    gather_across(4 + DN)
    pump_far(UP)
    for l in range(layers):
        k = 2 * l
        first = 4 * l
        need(first + QKV)
        attention_page(l, k, 0)
        rows_here(normed.at[k], k)
        if l == 0:
            attention_page(l, k, 1)
            need(OUT)
            sum_up_start(k, context_part(l))
            gather_start(4 + QKV)
            pump_near(UP)
            pump_far(DN)
        else:
            pump_near(4 + OUT)
            attention_page(l, k, 1)
            pump_near(4 + UP)
            pump_far(4 + DN)
            need(4 + OUT)
            sum_up_start(k, context_part(l))
            pump_near(4 + DN)
        v_buf[k + 1] = end_forward(k, k)
        norm_row(k + 1)
        k = k + 1
        if l == 0:
            pump_near(DN)
            pump_far(4 + QKV)
            gather_start(4 + OUT)
            gather_start(4 + UP)
        need(first + UP)
        mlp_page(l, k, 0)
        rows_here(normed.at[k], k)
        mlp_page(l, k, 1)
        if l == 0:
            need(DN)
            sum_up_start(k, hidden_part(l))
            pump_near(4 + QKV)
            pump_far(4 + OUT)
            pump_far(4 + UP)
            gather_start(4 + DN)
            v_buf[k + 1] = end_forward(k, k)
            norm_row(k + 1)

    both = 2 * prow

    def whole(ref):
        return ref.reshape(both, ref.shape[-1])

    def back_through_norm(k, g, ng):
        xhat, rr = norm_stats(v_buf[k].astype(F32))
        tiles[k, lay.gain_at : lay.gain_at + 1, :] = column_sum(ng * xhat)
        tiles[k, lay.shift_at : lay.shift_at + 1, :] = column_sum(ng)
        t = ng * vec(0, k)
        inner = t - jnp.mean(t, -1, keepdims=True) - xhat * jnp.mean(t * xhat, -1, keepdims=True)
        return g + rr * inner

    def scale_sum(k, g):
        tiles[k, lay.scale_at : lay.scale_at + 1, :] = column_sum(g * branch[k])

    def mlp_back(l, k, slot):
        dact = nt(bgrad[k, slot], weight("dn", l))
        gate[l, slot] = (dact * gate[l, slot].astype(F32)).astype(BF)

    def mlp_back_part(l):
        return lambda slot: nt(gate[l, slot], weight("up", l))

    def up_grads(l, k):
        dpre = whole(gate[l])
        keep_grad(4 * l + UP, tn(whole(normed[k]), dpre))
        sum_start(4 * l + UP)
        sec[lay.up_at + l : lay.up_at + l + 1, :] = column_sum(dpre.astype(F32))

    l, k = layers - 1, last
    rows_here(bgrad.at[k], halves + k)
    keep_grad(4 * l + DN, tn(whole(act[l]), whole(bgrad[k])))
    sum_start(4 * l + DN)
    need(4 * l + DN)
    mlp_back(l, k, 1)
    mlp_back(l, k, 0)
    sum_up_start(k, mlp_back_part(l))
    up_grads(l, k)
    sum_up_start(k + 1, hidden_part(l))
    g = back_through_norm(k, g4_buf[...], sum_up_end(k))
    g_buf[...] = g.astype(BF).astype(F32)

    def end_of_forward():
        after = end_forward(last, last + 1)
        scale_sum(last, g4_buf[...])
        if fused:
            share_page(after, "o_block")
        else:
            r.v4[...] = after

    for k in reversed(range(last)):
        l = k // 2
        step = 2 * halves - 1 - k
        g = g_buf[...]
        branch_grad(k, g)
        scale_sum(k, g)
        if k == last - 1:
            sum_first(4 * l + DN)
        if k % 2 == 0:

            def attention_back(slot):
                dctx = nt(bgrad[k, slot], weight("out", l)).astype(BF)
                for h in range(heads):
                    q = qkv[l, slot, :, h * hd : (h + 1) * hd]
                    kk = qkv[l, slot, :, own + h * hd : own + (h + 1) * hd]
                    vv = qkv[l, slot, :, 2 * own + h * hd : 2 * own + (h + 1) * hd]
                    dc = dctx[:, h * hd : (h + 1) * hd]
                    low_p = probs[l, slot, h]
                    p = low_p.astype(F32)
                    dp_ = nt(dc, vv)
                    ds = (p * (dp_ - jnp.sum(p * dp_, -1, keepdims=True))).astype(BF)
                    ds_ref[(l * heads + h) * 2 + slot, :, :prow] = ds.astype(F32)
                    dqkv[slot, :, h * hd : (h + 1) * hd] = (nn(ds, kk) * scale).astype(BF)
                    dqkv[slot, :, own + h * hd : own + (h + 1) * hd] = (tn(ds, q) * scale).astype(BF)
                    dqkv[slot, :, 2 * own + h * hd : 2 * own + (h + 1) * hd] = tn(low_p, dc).astype(BF)

            if l == 0:
                rows_here(bgrad.at[k], halves + k)
                keep_grad(OUT, tn(whole(ctx[l]), whole(bgrad[k])))
                sum_start(OUT)
                attention_back(0)
            else:
                attention_back(0)
                rows_here(bgrad.at[k], halves + k)
            attention_back(1)
            if l == 0:
                sum_second(4 + QKV)
                sum_second(4 + OUT)
            sum_up_start(step, lambda slot: nt(dqkv[slot], weight("qkv", l)))
            sum_first(4 * l + (UP if l > 0 else DN))
            dall = whole(dqkv[...])
            keep_grad(4 * l + QKV, tn(whole(normed[k]), dall))
            sum_start(4 * l + QKV)
            sums = column_sum(dall.astype(F32))
            sec[lay.qv_at + l : lay.qv_at + l + 1, :own] = sums[:, :own]
            sec[lay.qv_at + l : lay.qv_at + l + 1, 2 * LANES : 2 * LANES + own] = sums[:, 2 * own :]
            if l > 0:
                keep_grad(4 * l + OUT, tn(whole(ctx[l]), whole(bgrad[k])))
                sum_start(4 * l + OUT)
                end_of_forward()
                table_sums(l, 0, 2)
            else:
                sum_first(OUT)
                table_sums(l, 0, 2)
                sum_second(DN)
                table_sums(l, 1, 2)
        else:
            rows_here(bgrad.at[k], halves + k)
            keep_grad(4 * l + DN, tn(whole(act[l]), whole(bgrad[k])))
            sum_start(4 * l + DN)
            sum_second(4 * (l + 1) + DN)
            mlp_back(l, k, 1)
            mlp_back(l, k, 0)
            sum_up_start(step, mlp_back_part(l))
            up_grads(l, k)
            sum_second(4 * (l + 1) + UP)
            sum_first(4 * (l + 1) + QKV)
            table_sums(l + 1, 1, 2)
            sum_first(4 * (l + 1) + OUT)
        g = back_through_norm(k, g, sum_up_end(step))
        if k > 0:
            g_buf[...] = g.astype(BF).astype(F32)
    sum_first(UP)

    kept = jnp.where(masked, 0.0, g)
    token_sum = column_sum(jnp.where(masked, g, 0.0))
    for k in range(halves):
        tiles[k, lay.token_at : lay.token_at + 1, :] = token_sum
    for k in range(halves):
        share_rows(normed.at[k], k).wait_send()
        share_rows(bgrad.at[k], halves + k).wait_send()

    if not fused:
        r.g0[...] = kept
        return

    tile_copy = remote(tiles.at[mate_at], r.tile_in, r.small_s.at[0], r.small_r.at[0], mate)
    tile_copy.start()
    sent(tile_copy)
    red, red_in = r.red, r.red_in
    hops = [znear, zfar, xmate]

    def hop_copy(hop):
        return remote(red.at[hop], red_in.at[hop], r.small_s.at[1 + hop], r.small_r.at[1 + hop], hops[hop])

    def hop_start(hop):
        hop_copy(hop).start()
        sent(hop_copy(hop))

    def hop_end(hop):
        hop_copy(hop).wait_recv()
        red[hop + 1] = red[hop] + red_in[hop]

    share_page(kept, "o_input")
    finish_item(4 + DN)
    finish_item(4 + UP)
    tile_copy.wait_recv()
    red[0, :8] = tiles[section] + r.tile_in[...]
    red[0, 8:] = sec[...]
    hop_start(0)
    finish_item(4 + QKV)
    finish_item(4 + OUT)
    finish_item(DN)
    hop_end(0)
    hop_start(1)
    sum_second(UP)
    sum_first(QKV)
    sum_second(OUT)
    hop_end(1)
    hop_start(2)
    sum_second(QKV)
    finish_item(UP)
    hop_end(2)
    r.o_tile[...] = red[3, :8]
    sec_all, sec_sum = r.o_sec, r.sec_sum
    sec_sum[...] = red[3, 8:]
    sec_all[section] = sec_sum[...]
    for o in range(3):
        copy = remote(sec_sum, sec_all.at[section], r.sec_s.at[o], r.sec_r.at[o], sdev[o])
        copy.start()
        sent(copy)
    finish_item(OUT)
    finish_item(QKV)
    page_here("o_block")
    page_here("o_input")
    for n in reversed(range(4 * layers)):
        item_here(n)
    for o in range(3):
        remote(sec_sum, sec_all.at[sprev[o]], r.sec_s.at[o], r.sec_r.at[o], sdev[o]).wait_recv()
    for copy, when in sends:
        if when is None:
            copy.wait_send()
        else:
            pl.when(when)(copy.wait_send)


def run_blocks(lay, operands):
    L, prow, width, own, hid, shard = lay.layers, lay.prow, lay.width, lay.own, lay.hidden, lay.shard
    halves, steps, heads, pcol, page = lay.halves, 2 * lay.halves, lay.heads, lay.pcol, lay.rows
    rows = (prow, width)
    groups = 2 * heads
    dma = pltpu.SemaphoreType.DMA
    outs, scratch = {}, {}
    items = 4 * L
    wide = {"qkv": 3 * own, "up": hid, "dn": width, "out": width}
    raw = types.SimpleNamespace(**{name: (x.shape, x.dtype) for name, x in operands.items()})
    if lay.fused:
        outs.update(o_block=((2, prow, own), BF))
        outs.update(o_input=((2, prow, own), F32))
        outs.update(t_qkv=((L, 3, shard, own), BF))
        outs.update(t_out=((L, shard, own), BF))
        outs.update(t_up=((L, 4, shard, own), BF))
        outs.update(t_dn=((L, 4, shard, own), BF))
        outs.update(o_tile=((8, width), F32))
        outs.update(o_sec=((4, lay.sec_rows, width), F32))
        scratch.update(tiles=((halves, 8, width), F32))
        scratch.update(sec=((lay.sec_rows, width), F32))
        scratch.update(vec_all=((halves, 8, width), F32))
        scratch.update(vec_own=((8, width), F32))
        for kind, c in wide.items():
            lead = (2,) if kind == "out" else (2, 2, 2)
            scratch["w_" + kind] = ((L,) + lead + (shard, c), BF)
            scratch["g_" + kind] = ((L,) + lead + (shard, c), BF)
            scratch["x_" + kind] = ((L,) + (lead if kind == "out" else lead[:-1]) + (shard, c), BF)
            scratch["n_" + kind] = ((L,) + lead[:-2] + (shard, c), BF)
            scratch["f_" + kind] = ((L, shard, c), BF)
            scratch["s_" + kind] = ((L, 3 if kind == "qkv" else 4, shard, own), BF)
        scratch.update(a_qkv=((L, shard, 3 * own), BF))
        scratch.update(a_up=((L, shard, hid), BF))
        scratch.update(raw_qkv=(raw.qkv_weight, raw.up_weight)[0], raw_up=(raw.qkv_weight, raw.up_weight)[1])
        scratch.update(raw_qvb=(raw.qv_bias, raw.up_bias)[0], raw_upb=(raw.qv_bias, raw.up_bias)[1])
        scratch.update(raw_vec=((4,) + raw.ln_gain[0], BF))
        scratch.update(qvb=(((L, 3 * own), F32), ((L, hid), F32))[0], upb=(((L, 3 * own), F32), ((L, hid), F32))[1])
        scratch.update(o_block_s=(((4, prow, own), BF), ((4, prow, own), F32))[0], o_input_s=(((4, prow, own), BF), ((4, prow, own), F32))[1])
        scratch.update(tile_in=((8, width), F32))
        scratch.update(red=((4, 8 + lay.sec_rows, width), F32))
        scratch.update(red_in=((3, 8 + lay.sec_rows, width), F32))
        scratch.update(sec_sum=((lay.sec_rows, width), F32))
    else:
        outs.update(v4=(rows, BF))
        outs.update(g0=(rows, F32))
        outs.update(tiles=((halves, 8, width), F32))
        outs.update(sec=((lay.sec_rows, width), F32))
        outs.update(g_qkv=(((L, width, 3 * own), BF), ((L, own, width), BF))[0], g_out=(((L, width, 3 * own), BF), ((L, own, width), BF))[1])
        outs.update(g_up=(((L, width, hid), BF), ((L, hid, width), BF))[0], g_dn=(((L, width, hid), BF), ((L, hid, width), BF))[1])
    scratch.update(
        raw_x=raw.patches,
        raw_g=raw.cotangent,
        raw_mask=raw.page_mask,
        raw_token=raw.mask_token,
        raw_ids=raw.buckets,
        raw_table=raw.rel_table,
        ids=((prow, pcol), jnp.int32),
        table=((pad_up(L * heads, 8), lay.highs * LANES), F32),
        bias=((L * heads, prow, pcol), BF),
        v_buf=((halves,) + rows, BF),
        normed=((halves, 2) + rows, BF),
        branch=((halves,) + rows, F32),
        qkv=((L, 2, prow, 3 * own), BF),
        probs=((L, 2, heads, prow, prow), BF),
        ctx=((L, 2, prow, own), BF),
        act=((L, 2, prow, hid), BF),
        gate=((L, 2, prow, hid), BF),
        bgrad=((halves, 2) + rows, BF),
        dqkv=((2, prow, 3 * own), BF),
        acc=(rows, F32),
        g_buf=(rows, F32),
        g4_buf=(rows, F32),
        ds=((L * groups, prow, pcol), F32),
        hist=((lay.highs * groups, LANES), F32),
        core_out=((3,) + rows, BF),
        core_in=((3,) + rows, BF),
        far_out=((3,) + rows, BF),
        far_in=((3,) + rows, BF),
    )
    each = (steps,)
    sems = dict(core_s=each, core_r=each, far_s=each, far_r=each, row_s=each, row_r=each, load_s=(16,))
    if lay.fused:
        sems.update(
            ag_zfs=(items,), ag_zfr=(items,), ag_zns=(items,), ag_znr=(items,),
            ag_xs=(items, 3), ag_xr=(items, 3), ag_ls=(items,), vec_s=(3,), vec_r=(3,),
            rs_xs=(items,), rs_xr=(items,), rs_ns=(items,), rs_nr=(items,), rs_fs=(items,), rs_fr=(items,),
            rs_ss=(items, 3), rs_sr=(items, 3), page_s=(2,), page_r=(2,), small_s=(4,), small_r=(4,),
            sec_s=(3,), sec_r=(3,),
        )
    names = list(operands) + list(outs) + list(scratch) + list(sems)
    in_vmem = ("w_qkv", "w_out", "w_up", "w_dn", "vec_all", "qvb", "upb")
    spaces = [pltpu.VMEM if name in in_vmem else pl.ANY for name in operands]
    results = pl.pallas_call(
        functools.partial(blocks_kernel, lay, names),
        out_shape=tuple(jax.ShapeDtypeStruct(*spec) for spec in outs.values()),
        in_specs=[pl.BlockSpec(memory_space=space) for space in spaces],
        out_specs=[pl.BlockSpec(memory_space=pltpu.VMEM)] * len(outs),
        scratch_shapes=[pltpu.VMEM(*spec) for spec in scratch.values()] + [dma(spec) for spec in sems.values()],
        compiler_params=pltpu.CompilerParams(
            collective_id=1, has_side_effects=True, vmem_limit_bytes=61 * 2**20
        ),
        name="blocks",
        cost_estimate=pl.CostEstimate(flops=9 * 10**9, bytes_accessed=2 * 10**7, transcendentals=10**7),
    )(*operands.values())
    return dict(zip(outs, results))


def assemble_kernel(
    lay, block_ref, input_ref, qkv_ref, out_ref, up_ref, dn_ref, tile_ref, sec_ref,
    o_block, o_input, o_qkv, o_out, o_up, o_dn, o_qv, o_upb, o_table,
    o_gain, o_shift, o_scale, o_bias, o_token,
):
    rows, own, layers, heads = lay.rows, lay.own, lay.layers, lay.heads
    unit = own // 2
    for page in range(2):
        o_block[page] = block_ref[page].astype(F32).T[:, :rows].astype(BF)
        o_input[page] = input_ref[page].T[:, :rows]
    for l in range(layers):
        o_qkv[l] = jnp.concatenate([qkv_ref[l, place] for place in range(3)], 1).astype(F32)
        o_out[l] = out_ref[l].astype(F32)
        pieces = [up_ref[l, t, :, half * unit : (half + 1) * unit] for half in range(2) for t in range(4)]
        o_up[l] = jnp.concatenate(pieces, 1).astype(F32)
        o_dn[l] = dn_ref[l].reshape(4 * lay.shard, own).astype(F32).T
    q = [sec_ref[t, lay.qv_at : lay.qv_at + layers, :own] for t in range(4)]
    v = [sec_ref[t, lay.qv_at : lay.qv_at + layers, 2 * LANES : 2 * LANES + own] for t in range(4)]
    o_qv[...] = jnp.concatenate(q + v, 1)
    up = [sec_ref[t, lay.up_at : lay.up_at + layers, :] for t in range(4)]
    count = lay.hidden // unit
    o_upb[...] = jnp.concatenate([up[t][:, d * unit : (d + 1) * unit] for d in range(count) for t in range(4)], 1)
    buckets = o_table.shape[2]
    for l in range(layers):
        for t in range(4):
            at = lay.table_at + l * heads
            for h in range(heads):
                o_table[t * heads + h, l : l + 1, :] = sec_ref[t, at + h : at + h + 1, :buckets]
    for out, at in ((o_gain, lay.gain_at), (o_shift, lay.shift_at), (o_scale, lay.scale_at), (o_bias, lay.bias_at)):
        out[...] = tile_ref[at : at + 1, :]
    o_token[...] = tile_ref[lay.token_at, :]


def assemble(lay, bucket_count, res):
    L, own, width, hid, shard = lay.layers, lay.own, lay.width, lay.hidden, lay.shard
    row = ((1, width), F32)
    outs = [
        ((2, own, lay.rows), BF), ((2, own, lay.rows), F32),
        ((L, shard, 3 * own), F32), ((L, shard, own), F32), ((L, shard, hid), F32), ((L, own, 4 * shard), F32),
        ((L, 2 * width), F32), ((L, 4 * hid), F32), ((4 * lay.heads, L, bucket_count), F32),
        row, row, row, row, ((width,), F32),
    ]
    return pl.pallas_call(
        functools.partial(assemble_kernel, lay),
        out_shape=tuple(jax.ShapeDtypeStruct(*spec) for spec in outs),
        in_specs=[pl.BlockSpec(memory_space=pltpu.VMEM)] * len(res),
        name="assemble",
        cost_estimate=pl.CostEstimate(flops=10**6, bytes_accessed=4 * 10**6, transcendentals=0),
    )(*res.values())


def per_device(
    patches, page_mask, mask_token, buckets, ln_gain, ln_shift, layer_scale, branch_bias,
    qkv_weight, qv_bias, out_weight, rel_table, up_weight, up_bias, down_weight, cotangent,
):
    section = lax.axis_index("section")
    sections = lax.axis_size("section")
    ranks = lax.axis_size("dp")
    layers = qkv_weight.shape[0]
    pages, rows, width = patches.shape
    all_heads = rel_table.shape[1]
    bucket_count = rel_table.shape[2]
    head = width // all_heads
    heads = all_heads // sections
    own = heads * head
    hidden = up_weight.shape[2]
    hid = hidden // sections
    prow, pcol = pad_up(rows, 16), pad_up(rows, LANES)
    highs = pad_up(bucket_count, LANES) // LANES
    fused = ranks == 8 and sections == 4
    shard = qkv_weight.shape[1]
    lay = Layout(layers, heads, head, rows, prow, pcol, width, hid, shard, highs, fused)

    operands = dict(
        patches=patches.transpose(1, 0, 2), page_mask=page_mask, mask_token=mask_token,
        buckets=buckets, rel_table=rel_table.transpose(1, 0, 2), cotangent=cotangent.transpose(1, 0, 2),
    )
    if fused:
        operands.update(
            ln_gain=ln_gain, ln_shift=ln_shift, layer_scale=layer_scale, branch_bias=branch_bias,
            qkv_weight=qkv_weight, out_weight=out_weight, up_weight=up_weight, down_weight=down_weight,
            qv_bias=qv_bias, up_bias=up_bias,
        )
        out = list(assemble(lay, bucket_count, run_blocks(lay, operands)))
        for at in (0, 1, 5):
            out[at] = out[at].transpose(0, 2, 1)
        out[8] = out[8].transpose(1, 0, 2)
        return tuple(out)

    unit = down_weight.shape[1] // sections
    cols = width // sections

    def pick(x, axis):
        return lax.dynamic_index_in_dim(x, section, axis, keepdims=False)

    qkv_own = pick(qkv_weight.reshape(layers, shard, 3, sections, own), 3).reshape(layers, shard, 3 * own)
    up_own = pick(up_weight.reshape(layers, shard, ranks, sections, unit), 3).reshape(layers, shard, hid)
    dn_own = pick(down_weight.reshape(layers, sections, unit, width), 1)

    vecs = jnp.concatenate([ln_gain, ln_shift, layer_scale, branch_bias], 0).astype(F32)
    vecs = jnp.pad(vecs, ((0, 4), (0, 0)))
    qv_own = pick(qv_bias.reshape(layers, 2, sections, own), 2).astype(F32)
    qv_vec = jnp.concatenate([qv_own[:, 0], jnp.zeros_like(qv_own[:, 0]), qv_own[:, 1]], 1)
    upb_own = pick(up_bias.reshape(layers, ranks, sections, unit), 2).reshape(layers, hid).astype(F32)
    operands.update(qvb=qv_vec, upb=upb_own)

    def assembled(sec_all):
        qv = sec_all[:, lay.qv_at : lay.qv_at + layers]
        qv = jnp.stack([qv[..., :own], qv[..., 2 * LANES : 2 * LANES + own]], 2)
        qv = qv.transpose(1, 2, 0, 3).reshape(layers, 2 * width)
        up = sec_all[:, lay.up_at : lay.up_at + layers].reshape(sections, layers, ranks, unit)
        up = up.transpose(1, 2, 0, 3).reshape(layers, hidden)
        table = sec_all[:, lay.table_at : lay.table_at + layers * heads, :bucket_count]
        table = table.reshape(sections, layers, heads, bucket_count)
        return qv, up, table.transpose(1, 0, 2, 3).reshape(layers, all_heads, bucket_count)

    def gathered(x):
        return lax.all_gather(x, "dp", axis=1, tiled=True)

    operands.update(
        vec_all=lax.all_gather(vecs, "section", axis=0, tiled=False),
        w_qkv=gathered(qkv_own),
        w_out=pick(gathered(out_weight).reshape(layers, sections, own, width), 1),
        w_up=gathered(up_own),
        w_dn=gathered(dn_own),
    )
    res = run_blocks(lay, operands)

    def scattered(x):
        return lax.psum_scatter(x, "dp", scatter_dimension=1, tiled=True)

    def everywhere(x, axis):
        return lax.all_gather(x, "section", axis=axis, tiled=False)

    sqkv, sup, sdn = scattered(res["g_qkv"]), scattered(res["g_up"]), scattered(res["g_dn"])
    qkv_all = everywhere(sqkv.reshape(layers, shard, 3, own), 3).reshape(layers, shard, 3 * width)
    qkv_cols = 3 * width // sections
    qkv_out = lax.dynamic_slice_in_dim(qkv_all, section * qkv_cols, qkv_cols, 2).astype(F32)
    up_all = everywhere(sup.reshape(layers, shard, ranks, unit), 3).reshape(layers, shard, hidden)
    up_out = lax.dynamic_slice_in_dim(up_all, section * hid, hid, 2).astype(F32)
    dn_all = lax.all_to_all(
        sdn.reshape(layers, unit, sections, cols), "section", split_axis=2, concat_axis=1, tiled=False
    )
    dn_out = dn_all.reshape(layers, sections * unit, cols).astype(F32)
    out_mine = scattered(everywhere(res["g_out"], 1).reshape(layers, width, width))
    out_out = lax.dynamic_slice_in_dim(out_mine, section * cols, cols, 2).astype(F32)

    def pages_of(x):
        both = lax.all_gather(x[:rows], "section", axis=0, tiled=False)[:pages]
        return lax.dynamic_slice_in_dim(both, section * cols, cols, 2)

    once = (section < 2).astype(F32)
    here = (jnp.arange(sections) == section).astype(F32)
    tiles, sec_all = lax.psum(
        (res["tiles"] * once, res["sec"][None] * here[:, None, None]), ("section", "dp")
    )
    tile = pick(tiles, 0)
    return (
        pages_of(res["v4"]), pages_of(res["g0"]), qkv_out, out_out, up_out, dn_out,
        *assembled(sec_all),
        *[tile[at : at + 1] for at in (lay.gain_at, lay.shift_at, lay.scale_at, lay.bias_at)],
        tile[lay.token_at],
    )


def solution(mesh):
    rows3 = P("dp", None, None)
    part = P("section", None)
    weight = P(None, "dp", None)
    in_specs = (
        rows3, P("dp", None), P(), P(), part, part, part, part,
        weight, P(), weight, P(), weight, P(), weight, rows3,
    )
    cut = P("dp", None, "section")
    grad = P(None, "dp", "section")
    out_specs = (cut, cut, grad, grad, grad, grad, P(), P(), P(), part, part, part, part, P())
    return jax.shard_map(per_device, mesh=mesh, in_specs=in_specs, out_specs=out_specs, check_vma=False)
```

profile of v0, /device:TPU:0, one launch (start us, length us, event | category | flops | bytes accessed | tf_op | source)
XLA Modules:
  0.0 200.9 jit_solution(15848893705568965073)
XLA Ops:
  0.7 196.8 %blocks.1 = (bf16[2,208,192]{2,1,0:T(8,128)(2,1)}, f32[2,208,192]{2,1,0:T(8,128)}, bf16[2,3,96,192]{3,2,1,0:T(8,128)(2,1)}, bf16[2,96,192]{2,1,0:T(8,128)(2,1)},...) custom-call(bf16[197,2,768]{2,1,0:T(2,128)(2,1)} %bitcast.7, ...), custom_call_target="tpu_custom_call" | custom-call | flops 8999999488 | bytes 20000000 | tf_op jit(solution)/shard_map/blocks/pallas_call | solution.py:962
  197.4 3.3 %assemble.1 = (bf16[2,192,197]{2,1,0:T(8,128)(2,1)}, f32[2,192,197]{2,1,0:T(8,128)}, f32[2,96,576]{2,1,0:T(8,128)}, f32[2,96,192]{2,1,0:T(8,128)}, f32[2,96,768]...) custom-call(bf16[2,208,192]{2,1,0:T(8,128)(2,1)} %get-tuple-element., ...), custom_call_target="tpu_custom_call" | custom-call | flops 1000000 | bytes 4000000 | tf_op jit(solution)/shard_map/assemble/pallas_call | solution.py:1019
where the time goes:
time: 201 us
  Pallas kernels  200 us (100%)
    pallas_call x1, Pallas kernels, run_blocks(): pl.pallas_call(functools.partial(blocks_kernel, lay, names), out_shape=tu...  197 us

commit v1 on v0

--- a/solution.py
+++ b/solution.py
@@ -636,38 +636,38 @@
         rows_here(normed.at[k], k)
         if l == 0:
             attention_page(l, k, 1)
+            gather_start(4 + QKV)
             need(OUT)
             sum_up_start(k, context_part(l))
-            gather_start(4 + QKV)
             pump_near(UP)
             pump_far(DN)
+            gather_start(4 + OUT)
+            gather_start(4 + UP)
         else:
-            pump_near(4 + OUT)
             attention_page(l, k, 1)
-            pump_near(4 + UP)
-            pump_far(4 + DN)
+            pump_near(4 + DN)
             need(4 + OUT)
             sum_up_start(k, context_part(l))
-            pump_near(4 + DN)
         v_buf[k + 1] = end_forward(k, k)
         norm_row(k + 1)
         k = k + 1
         if l == 0:
             pump_near(DN)
             pump_far(4 + QKV)
-            gather_start(4 + OUT)
-            gather_start(4 + UP)
+            gather_start(4 + DN)
         need(first + UP)
         mlp_page(l, k, 0)
         rows_here(normed.at[k], k)
         mlp_page(l, k, 1)
         if l == 0:
+            pump_far(4 + OUT)
+            pump_far(4 + UP)
             need(DN)
             sum_up_start(k, hidden_part(l))
             pump_near(4 + QKV)
-            pump_far(4 + OUT)
-            pump_far(4 + UP)
-            gather_start(4 + DN)
+            pump_near(4 + OUT)
+            pump_far(4 + DN)
+            pump_near(4 + UP)
             v_buf[k + 1] = end_forward(k, k)
             norm_row(k + 1)
 
@@ -720,6 +720,16 @@
             share_page(after, "o_block")
         else:
             r.v4[...] = after
+
+    forward_sends = len(sends)
+
+    def drain(count):
+        for copy, when in sends[:count]:
+            if when is None:
+                copy.wait_send()
+            else:
+                pl.when(when)(copy.wait_send)
+        del sends[:count]
 
     for k in reversed(range(last)):
         l = k // 2
@@ -774,9 +784,7 @@
                 table_sums(l, 0, 2)
             else:
                 sum_first(OUT)
-                table_sums(l, 0, 2)
-                sum_second(DN)
-                table_sums(l, 1, 2)
+                table_sums(l, 0, 1)
         else:
             rows_here(bgrad.at[k], halves + k)
             keep_grad(4 * l + DN, tn(whole(act[l]), whole(bgrad[k])))
@@ -789,6 +797,8 @@
             sum_second(4 * (l + 1) + UP)
             sum_first(4 * (l + 1) + QKV)
             table_sums(l + 1, 1, 2)
+            drain(forward_sends)
+            early_sends = len(sends)
             sum_first(4 * (l + 1) + OUT)
         g = back_through_norm(k, g, sum_up_end(step))
         if k > 0:
@@ -831,18 +841,20 @@
     red[0, :8] = tiles[section] + r.tile_in[...]
     red[0, 8:] = sec[...]
     hop_start(0)
+    sum_second(DN)
     finish_item(4 + QKV)
     finish_item(4 + OUT)
-    finish_item(DN)
+    sum_first(QKV)
     hop_end(0)
     hop_start(1)
     sum_second(UP)
-    sum_first(QKV)
+    finish_item(DN)
     sum_second(OUT)
+    sum_second(QKV)
     hop_end(1)
     hop_start(2)
-    sum_second(QKV)
     finish_item(UP)
+    drain(early_sends)
     hop_end(2)
     r.o_tile[...] = red[3, :8]
     sec_all, sec_sum = r.o_sec, r.sec_sum
@@ -860,11 +872,7 @@
         item_here(n)
     for o in range(3):
         remote(sec_sum, sec_all.at[sprev[o]], r.sec_s.at[o], r.sec_r.at[o], sdev[o]).wait_recv()
-    for copy, when in sends:
-        if when is None:
-            copy.wait_send()
-        else:
-            pl.when(when)(copy.wait_send)
+    drain(len(sends))
 
 
 def run_blocks(lay, operands):

time: 201 us -> 195 us (0.970)
  Pallas kernels: 200 us -> 194 us
    pallas_call x1, Pallas kernels: 197 us -> 191 us  [run_blocks(): pl.pallas_call(functools.partial(blocks_kernel, lay, names), out_shape=tu...]
where the time goes in v1:
time: 195 us
  Pallas kernels  194 us (99%)
    pallas_call x1, Pallas kernels, run_blocks(): pl.pallas_call(functools.partial(blocks_kernel, lay, names), out_shape=tu...  191 us

profile of v1, /device:TPU:0, one launch (start us, length us, event | category | flops | bytes accessed | tf_op | source)
XLA Modules:
  0.0 195.0 jit_solution(13690331320044663371)
XLA Ops:
  0.7 190.9 %blocks.1 = (bf16[2,208,192]{2,1,0:T(8,128)(2,1)}, f32[2,208,192]{2,1,0:T(8,128)}, bf16[2,3,96,192]{3,2,1,0:T(8,128)(2,1)}, bf16[2,96,192]{2,1,0:T(8,128)(2,1)},...) custom-call(bf16[197,2,768]{2,1,0:T(2,128)(2,1)} %bitcast.7, ...), custom_call_target="tpu_custom_call" | custom-call | flops 8999999488 | bytes 20000000 | tf_op jit(solution)/shard_map/blocks/pallas_call | solution.py:970
  191.5 3.3 %assemble.1 = (bf16[2,192,197]{2,1,0:T(8,128)(2,1)}, f32[2,192,197]{2,1,0:T(8,128)}, f32[2,96,576]{2,1,0:T(8,128)}, f32[2,96,192]{2,1,0:T(8,128)}, f32[2,96,768]...) custom-call(bf16[2,208,192]{2,1,0:T(8,128)(2,1)} %get-tuple-element., ...), custom_call_target="tpu_custom_call" | custom-call | flops 1000000 | bytes 4000000 | tf_op jit(solution)/shard_map/assemble/pallas_call | solution.py:1027
